TPU v7x, 512 devices: a whole 4x8x8 slice. The times are simulated.
512 devices in a mesh: seq: 64 (over z, x, y_lo), tp: 8 (over y_hi, core).
Axes of the slice: x: 4, y: 8 (y_hi: 4, y_lo: 2; y = y_hi * 2 + y_lo), z: 8, core: 2. Of those that a mesh axis runs over, the one named last changes fastest.
Arguments:
- tokens: bfloat16 [16384, 3200], P('seq'), may hold values from -8 to 8
- norm_gain: float32 [3200], replicated, may hold values from 0.5 to 1.5
- qkv_weight: bfloat16 [3200, 3, 2048], P('seq', None, 'tp'), may hold values from -1 to 1
- q_gain: float32 [2048], P('tp'), may hold values from 0.5 to 5, as said below
- k_gain: float32 [2048], P('tp'), may hold values from 0.5 to 5, as said below
- out_weight: bfloat16 [2048, 3200], P('tp', 'seq'), may hold values from -0.125 to 0.125
- layer_scale: float32 [3200], P('tp'), may hold values from 0.5 to 2
- segment_ids: int32 [16384], replicated, may hold values from 0 to 63, never falling along the last dimension, each value on 1 to 512 neighbouring positions
Outputs:
- mixed: bfloat16 [16384, 3200], P('seq', 'tp')
Inputs may be any that keep to these rules, and one draw needn't show every extreme that they name: `segment_ids`: image numbers never fall along the row; each image has 1 to 512 patches, one exactly 512. `q_gain`: positive gains. `k_gain`: positive gains.
All inputs are finite; a program needn't handle non-finite values.
Results may differ from a plain program's by a relative error of at most 0.0078.
Values may be sent and summed in bfloat16 or wider, within the bound.
A program may use at most 64 MiB of HBM per device.

v0:
```python
import jax
import jax.numpy as jnp
from jax import lax
from jax.sharding import PartitionSpec as P

HEAD_DIM = 128
eps = 1e-06
floor_score = -1e30


def passed_along(x, axis, by):
    size = lax.axis_size(axis)
    pairs = [(i, i + by) for i in range(size) if 0 <= i + by < size]
    return lax.ppermute(x, axis, pairs)


def masked_scores(query, keys, query_seg, key_seg):
    scores = jnp.einsum(
        "qhd,khd->hqk", query, keys, preferred_element_type=jnp.float32
    ) * HEAD_DIM ** (-0.5)
    mask = (query_seg[:, None] == key_seg[None, :])[None]
    return (jnp.where(mask, scores, floor_score), mask)


def shards(tokens, norm_gain, qkv_weight, q_gain, k_gain, out_weight, layer_scale, segment_ids):
    count = tokens.shape[0]
    source = tokens.astype(jnp.float32)
    normed = (
        source * lax.rsqrt(jnp.mean(source * source, axis=-1, keepdims=True) + eps) * norm_gain
    ).astype(jnp.bfloat16)
    local_width = qkv_weight.shape[2]
    heads = local_width // HEAD_DIM
    joined = jnp.einsum(
        "td,dch->tch",
        normed,
        lax.all_gather(qkv_weight, "seq", axis=0, tiled=True),
        preferred_element_type=jnp.float32,
    )
    query = joined[:, 0]
    keys = joined[:, 1]
    values = joined[:, 2]
    query_sq, key_sq = lax.psum(
        (jnp.sum(query * query, axis=-1), jnp.sum(keys * keys, axis=-1)), "tp"
    )
    full_width = local_width * lax.axis_size("tp")
    query_normed = (query * lax.rsqrt(query_sq / full_width + eps)[:, None] * q_gain).astype(
        jnp.bfloat16
    )
    key_normed = (keys * lax.rsqrt(key_sq / full_width + eps)[:, None] * k_gain).astype(
        jnp.bfloat16
    )
    paired = jnp.stack([key_normed, values.astype(jnp.bfloat16)], axis=1)
    pieces = []
    for offset in (2, 1, 0, -1, -2):
        if offset == 0:
            pieces.append(paired)
        else:
            pieces.append(passed_along(paired, "seq", offset))
    widened = jnp.concatenate(pieces, axis=0)
    position = lax.axis_index("seq")
    outside = jnp.full((2 * count,), -1, jnp.int32)
    seg_pad = jnp.concatenate([outside, segment_ids, outside], axis=0)
    key_seg = lax.dynamic_slice_in_dim(seg_pad, position * count, 5 * count, 0)
    query_seg = lax.dynamic_slice_in_dim(segment_ids, position * count, count, 0)
    query_heads = query_normed.reshape(count, heads, HEAD_DIM)
    key_heads = widened[:, 0].reshape(5 * count, heads, HEAD_DIM)
    value_heads = widened[:, 1].reshape(5 * count, heads, HEAD_DIM)
    scores, mask = masked_scores(query_heads, key_heads, query_seg, key_seg)
    peak = jnp.max(scores, axis=-1, keepdims=True)
    weights = jnp.where(mask, jnp.exp(scores - peak), 0.0)
    total = jnp.sum(weights, axis=-1)
    probs = weights.astype(jnp.bfloat16)
    summed = jnp.einsum("hqk,khd->qhd", probs, value_heads, preferred_element_type=jnp.float32)
    context = (
        (summed / jnp.transpose(total)[:, :, None]).reshape(count, local_width).astype(jnp.bfloat16)
    )
    terms = jnp.dot(
        context,
        lax.all_gather(out_weight, "seq", axis=1, tiled=True),
        preferred_element_type=jnp.float32,
    )
    projected = lax.psum_scatter(terms, "tp", scatter_dimension=1, tiled=True)
    share = layer_scale.shape[0]
    residual = lax.dynamic_slice_in_dim(source, lax.axis_index("tp") * share, share, 1)
    return (residual + layer_scale * projected).astype(jnp.bfloat16)


def solution(mesh):
    return jax.shard_map(
        shards,
        mesh=mesh,
        in_specs=(
            P("seq", None),
            P(),
            P("seq", None, "tp"),
            P("tp"),
            P("tp"),
            P("tp", "seq"),
            P("tp"),
            P(),
        ),
        out_specs=P("seq", "tp"),
        check_vma=False,
    )
```

profile of v0, /device:TPU:27, one launch (start us, length us, event | category | flops | bytes accessed | tf_op | source)
XLA Modules:
  0.0 731.3 jit_solution(13992945000066790552)
XLA Ops:
  6.5 1.6 copy.18
  9.0 3.0 copy.17
  12.6 278.7 %all-gather.4.cloned.1.call-done = bf16[3200,3,256]{2,1,0:T(4,128)(2,1)} async-done(((bf16[50,3,256]{2,1,0:T(4,128)(2,1)}), bf16[3200,3,256]{2,1,0:T(4,128)(2,1)}) %all-gather.4.cloned.1.call-update) | async-done | bytes 4915216 | tf_op jit(solution)/shard_map/all_gather | solution.py:36
  291.3 5.3 fusion.1
  296.7 55.5 %all-reduce = (f32[256]{0:T(256)S(1)}, f32[256]{0:T(256)S(1)}) all-reduce(f32[256]{0:T(256)S(1)} %get-tuple-element.6, f32[256]{0:T(256)S(1)} %get-tuple-element.5), channel_id=1, replica_groups=mesh['seq'=64,'tp'=8] {'tp'}, use_global_device_ids=true, to_apply=%region_2.0 | all-reduce | flops 512 | bytes 4096 | tf_op jit(solution)/shard_map/psum | solution.py:42
  353.7 1.9 collective-permute-start
  355.6 1.0 broadcast_compare_fusion
  356.6 233.7 %all-gather.6.cloned.1.call-done = bf16[64,50,256]{2,1,0:T(8,128)(2,1)} async-done(((bf16[1,50,256]{2,1,0:T(8,128)(2,1)}), bf16[64,50,256]{2,1,0:T(8,128)(2,1)}) %all-gather.6.cloned.1.call-update) | async-done | bytes 1638416 | tf_op jit(solution)/shard_map/all_gather | solution.py:79
  590.3 2.5 reshape.70
  592.8 4.8 collective-permute-start.1
  597.6 5.0 collective-permute-start.2
  602.7 3.1 collective-permute-start.3
  605.8 1.8 copy.21
  607.5 1.7 multiply_convert_fusion.1
  610.2 1.0 constant_dynamic-update-slice_fusion.3
  611.3 1.0 constant_dynamic-update-slice_fusion.1
  612.3 1.0 constant_dynamic-update-slice_fusion
  613.2 1.2 fusion.34
  614.4 2.6 fusion.36
  617.1 2.8 fusion.20
  619.9 2.3 fusion.37
  622.2 2.0 convert_element_type.28
  624.2 98.7 %reduce-scatter.2.cloned.1.call-done = f32[256,400]{0,1:T(8,128)} async-done(((f32[256,3200]{0,1:T(8,128)}), f32[256,400]{0,1:T(8,128)}) %reduce-scatter.2.cloned.1.call-update) | async-done | bytes 409616 | tf_op jit(solution)/shard_map/reduce_scatter | solution.py:82
  722.9 1.9 add_convert_fusion
  (34 shorter events, 4.0 us)
Async XLA Ops:
  6.5 5.4 copy-start.1
  6.5 284.8 %all-gather.4.cloned.1.call-start = ((), (), s32[]{:S(2)}) async-start(), calls=%async_computation.1 | async-start | bytes 6656000 | tf_op jit(solution)/shard_map/all_gather | solution.py:36
  8.1 283.2 %copy-start.5 = (f32[3200]{0:T(1024)S(1)}, f32[3200]{0:T(1024)}, u32[]{:S(2)}) copy-start(f32[3200]{0:T(1024)} %param.9) | copy-start | bytes 38404
  8.2 582.1 %all-gather.6.cloned.1.call-start = ((), (), s32[]{:S(2)}) async-start(), calls=%async_computation.3 | async-start | bytes 1863680 | tf_op jit(solution)/shard_map/all_gather | solution.py:79
  8.9 713.9 %reduce-scatter.2.cloned.1.call-start = ((), (), s32[]{:S(2)}) async-start(), calls=%async_computation.2 | async-start | bytes 3686400 | tf_op jit(solution)/shard_map/reduce_scatter | solution.py:82
  12.6 339.6 %copy-start.3 = (f32[256]{0:T(256)S(1)}, f32[256]{0:T(256)}, u32[]{:S(2)}) copy-start(f32[256]{0:T(256)} %param.12) | copy-start | bytes 3076
  352.9 254.6 %copy-start.4 = (f32[256]{0:T(256)S(1)}, f32[256]{0:T(256)}, u32[]{:S(2)}) copy-start(f32[256]{0:T(256)} %param.11) | copy-start | bytes 3076
  353.7 255.6 %collective-permute-start = (bf16[256,2,256]{0,2,1:T(8,128)(2,1)}, bf16[256,2,256]{0,2,1:T(8,128)(2,1)}, u32[]{:S(2)}, u32[]{:S(2)}) collective-permute-start(bf16[256,2,256]{0,2,1:T(8,128)(2,1)} %pad_maximum_fusion), channel_id=1, source_target_pairs={{0,16},{8,24},{16,32},{24,40},{32,48},{40,56},{48,64},{56,72},{64,... | collective-permute-start | bytes 786440 | tf_op jit(solution)/shard_map/ppermute | solution.py:14
  592.8 17.5 %collective-permute-start.1 = (bf16[256,2,256]{0,2,1:T(8,128)(2,1)}, bf16[256,2,256]{0,2,1:T(8,128)(2,1)}, u32[]{:S(2)}, u32[]{:S(2)}) collective-permute-start(bf16[256,2,256]{0,2,1:T(8,128)(2,1)} %pad_maximum_fusion), channel_id=1, source_target_pairs={{0,8},{8,16},{16,24},{24,32},{32,40},{40,48},{48,56},{56,64},{64,7... | collective-permute-start | bytes 786440 | tf_op jit(solution)/shard_map/ppermute | solution.py:14
  597.6 13.6 %collective-permute-start.2 = (bf16[256,2,256]{0,2,1:T(8,128)(2,1)}, bf16[256,2,256]{0,2,1:T(8,128)(2,1)}, u32[]{:S(2)}, u32[]{:S(2)}) collective-permute-start(bf16[256,2,256]{0,2,1:T(8,128)(2,1)} %pad_maximum_fusion), channel_id=1, source_target_pairs={{8,0},{16,8},{24,16},{32,24},{40,32},{48,40},{56,48},{64,56},{72,6... | collective-permute-start | bytes 786440 | tf_op jit(solution)/shard_map/ppermute | solution.py:14
  602.7 9.6 %collective-permute-start.3 = (bf16[256,2,256]{0,2,1:T(8,128)(2,1)}, bf16[256,2,256]{0,2,1:T(8,128)(2,1)}, u32[]{:S(2)}, u32[]{:S(2)}) collective-permute-start(bf16[256,2,256]{0,2,1:T(8,128)(2,1)} %pad_maximum_fusion), channel_id=1, source_target_pairs={{16,0},{24,8},{32,16},{40,24},{48,32},{56,40},{64,48},{72,56},{80,... | collective-permute-start | bytes 786440 | tf_op jit(solution)/shard_map/ppermute | solution.py:14
  611.2 3.2 copy-start
  622.2 100.7 %copy-start.2 = (f32[400]{0:T(512)S(1)}, f32[400]{0:T(512)}, u32[]{:S(2)}) copy-start(f32[400]{0:T(512)} %param.14) | copy-start | bytes 4804
Sparse Core Ops, SparseCore 0:
  9.4 281.8 all-gather.3
  293.4 296.8 all-gather.5
  622.3 100.5 reduce-scatter.1
where the time goes:
time: 732 us; the launch traced here: 731 us
  waiting for transfers between devices  612 us (84%)
  blocking collectives  55.5 us (8%)
  starting transfers between devices  14.9 us (2%)
  local copies, waits for them, and re-layouts  14.1 us (2%)
  between operations  13.3 us (2%)
  matrix products  13.1 us (2%)
  other arithmetic  8.7 us (1%)
    all_gather x1, waiting for transfers between devices, shards(): lax.all_gather(qkv_weight, 'seq', axis=0, tiled=True)  279 us
    all_gather x1, waiting for transfers between devices, shards(): lax.all_gather(out_weight, 'seq', axis=1, tiled=True)  234 us
    reduce_scatter x1, waiting for transfers between devices, shards(): projected = lax.psum_scatter(terms, 'tp', scatter_dimension=1, tiled=True)  98.7 us
    psum x1, blocking collectives, shards(): lax.psum((jnp.sum(query * query, axis=-1), jnp.sum(keys * keys, axis=-1))...  55.5 us
    ppermute x4, starting transfers between devices, passed_along(): return lax.ppermute(x, axis, pairs)  14.9 us
  transfers between devices with their start and end apart: 7, of which 3 were waited for; matrix products, arithmetic and copies ran while one was open for 3% of the time, Pallas kernels for 0%

commit v1 on v0

--- a/solution.py
+++ b/solution.py
@@ -33,7 +33,9 @@
     joined = jnp.einsum(
         "td,dch->tch",
         normed,
-        lax.all_gather(qkv_weight, "seq", axis=0, tiled=True),
+        jnp.concatenate(
+            lax.all_to_all(jnp.stack([qkv_weight] * lax.axis_size("seq")), "seq", 0, 0), axis=0
+        ),
         preferred_element_type=jnp.float32,
     )
     query = joined[:, 0]

time: 732 us -> 434 us (0.59)
  the two profiles are of different devices: /device:TPU:27 before, /device:TPU:31 now
where the time goes in v1:
time: 434 us; the launch traced here: 433 us
  waiting for transfers between devices  325 us (75%)
  starting transfers between devices  30.7 us (7%)
  local copies, waits for them, and re-layouts  28.4 us (7%)
  blocking collectives  13.7 us (3%)
  between operations  13.6 us (3%)
  matrix products  12.6 us (3%)
  other arithmetic  8.7 us (2%)
    all_to_all x1, waiting for transfers between devices, shards(): lax.all_to_all(jnp.stack([qkv_weight] * lax.axis_size('seq')), 'seq', 0, 0)  123 us
    reduce_scatter x1, waiting for transfers between devices, shards(): projected = lax.psum_scatter(terms, 'tp', scatter_dimension=1, tiled=True)  103 us
    all_gather x1, waiting for transfers between devices, shards(): lax.all_gather(out_weight, 'seq', axis=1, tiled=True)  97.7 us
    ppermute x4, starting transfers between devices, passed_along(): return lax.ppermute(x, axis, pairs)  16.2 us
    all_to_all x1, starting transfers between devices, shards(): lax.all_to_all(jnp.stack([qkv_weight] * lax.axis_size('seq')), 'seq', 0, 0)  14.4 us
    psum x1, blocking collectives, shards(): lax.psum((jnp.sum(query * query, axis=-1), jnp.sum(keys * keys, axis=-1))...  13.7 us
  transfers between devices with their start and end apart: 7, of which 3 were waited for; matrix products, arithmetic and copies ran while one was open for 8% of the time, Pallas kernels for 0%

profile of v1, /device:TPU:31, one launch (start us, length us, event | category | flops | bytes accessed | tf_op | source)
XLA Modules:
  0.0 432.7 jit_solution(18417668391926173157)
XLA Ops:
  6.5 3.7 stack.4
  10.2 14.4 %all-to-all-start = ((bf16[64,50,3,256]{3,1,2,0:T(8,128)(2,1)}), bf16[64,50,3,256]{3,1,2,0:T(8,128)(2,1)}, u32[]{:S(2)}, u32[]{:S(2)}) async-start(bf16[64,50,3,256]{3,1,2,0:T(8,128)(2,1)} %stack.4), calls=%async_computation | async-start | bytes 11010048 | tf_op jit(solution)/shard_map/all_to_all | solution.py:37
  25.5 1.5 copy.19
  27.7 123.2 %all-to-all-done = bf16[64,50,3,256]{3,1,2,0:T(8,128)(2,1)} async-done(((bf16[64,50,3,256]{3,1,2,0:T(8,128)(2,1)}), bf16[64,50,3,256]{3,1,2,0:T(8,128)(2,1)}, u32[]{:S(2)}, u32[]{:S(2)}) %all-to-all-start) | async-done | bytes 4915232 | tf_op jit(solution)/shard_map/all_to_all | solution.py:37
  150.8 5.4 %copy.20 = bf16[64,50,3,256]{3,1,0,2:T(8,128)(2,1)} copy(bf16[64,50,3,256]{3,1,2,0:T(8,128)(2,1)} %all-to-all-done) | data formatting | bytes 9830400 | tf_op jit(solution)/shard_map/all_to_all | solution.py:37
  156.2 8.3 %reshape.74 = bf16[3200,3,256]{2,0,1:T(8,128)(2,1)} reshape(bf16[64,50,3,256]{3,1,0,2:T(8,128)(2,1)} %copy.20) | data formatting | bytes 9830400 | tf_op jit(solution)/shard_map/reshape | solution.py:36
  164.6 4.9 %fusion.6 = f32[256,3,256]{0,2,1:T(8,128)S(1)} fusion(bf16[3200,3,256]{2,0,1:T(8,128)(2,1)} %reshape.74, f32[3200]{0:T(1024)S(1)} %copy-done.6, f32[256]{0:T(256)S(1)} %add_rsqrt_fusion.2, bf16[256,3200]{0,1:T(8,128)(2,1)S(1)} %copy.19), kind=kOutput, calls=%fused_computation.9 | convolution fusion | flops 1261568000 | bytes 7353856 | tf_op jit(solution)/shard_map/td,dch->tch/dot_general | solution.py:33
  169.5 13.7 %all-reduce = (f32[256]{0:T(256)S(1)}, f32[256]{0:T(256)S(1)}) all-reduce(f32[256]{0:T(256)S(1)} %get-tuple-element.6, f32[256]{0:T(256)S(1)} %get-tuple-element.5), channel_id=1, replica_groups=mesh['seq'=64,'tp'=8] {'tp'}, use_global_device_ids=true, to_apply=%region_2.0 | all-reduce | flops 512 | bytes 4096 | tf_op jit(solution)/shard_map/psum | solution.py:44
  184.7 3.7 collective-permute-start
  189.4 97.7 %all-gather.3.cloned.1.call-done = bf16[64,50,256]{2,1,0:T(8,128)(2,1)} async-done(((bf16[1,50,256]{2,1,0:T(8,128)(2,1)}), bf16[64,50,256]{2,1,0:T(8,128)(2,1)}) %all-gather.3.cloned.1.call-update) | async-done | bytes 1638416 | tf_op jit(solution)/shard_map/all_gather | solution.py:81
  287.2 2.5 reshape.76
  289.7 3.8 collective-permute-start.1
  293.4 2.8 collective-permute-start.2
  296.2 6.0 %collective-permute-start.3 = (bf16[256,2,256]{0,2,1:T(8,128)(2,1)}, bf16[256,2,256]{0,2,1:T(8,128)(2,1)}, u32[]{:S(2)}, u32[]{:S(2)}) collective-permute-start(bf16[256,2,256]{0,2,1:T(8,128)(2,1)} %pad_maximum_fusion), channel_id=1, source_target_pairs={{16,0},{24,8},{32,16},{40,24},{48,32},{56,40},{64,48},{72,56},{80,... | collective-permute-start | bytes 786440 | tf_op jit(solution)/shard_map/ppermute | solution.py:14
  302.2 1.8 copy.23
  304.0 1.7 multiply_convert_fusion.1
  307.7 1.0 constant_dynamic-update-slice_fusion.1
  309.7 1.2 fusion.33
  310.8 2.6 fusion.35
  313.5 2.8 fusion.19
  316.3 2.3 fusion.36
  318.6 2.0 convert_element_type.28
  320.6 103.3 %reduce-scatter.2.cloned.1.call-done = f32[256,400]{0,1:T(8,128)} async-done(((f32[256,3200]{0,1:T(8,128)}), f32[256,400]{0,1:T(8,128)}) %reduce-scatter.2.cloned.1.call-update) | async-done | bytes 409616 | tf_op jit(solution)/shard_map/reduce_scatter | solution.py:84
  423.9 1.9 add_convert_fusion
  (37 shorter events, 6.9 us)
Async XLA Ops:
  10.2 15.3 %copy-start = (bf16[256,3200]{1,0:T(8,128)(2,1)S(1)}, bf16[256,3200]{1,0:T(8,128)(2,1)}, u32[]{:S(2)}) copy-start(bf16[256,3200]{1,0:T(8,128)(2,1)} %param.8) | copy-start | bytes 4915204
  10.2 140.6 %all-to-all-start = ((bf16[64,50,3,256]{3,1,2,0:T(8,128)(2,1)}), bf16[64,50,3,256]{3,1,2,0:T(8,128)(2,1)}, u32[]{:S(2)}, u32[]{:S(2)}) async-start(bf16[64,50,3,256]{3,1,2,0:T(8,128)(2,1)} %stack.4), calls=%async_computation | async-start | bytes 11010048 | tf_op jit(solution)/shard_map/all_to_all | solution.py:37
  24.7 2.3 copy-start.2
  24.7 262.5 %all-gather.3.cloned.1.call-start = ((), (), s32[]{:S(2)}) async-start(), calls=%async_computation.3 | async-start | bytes 1863680 | tf_op jit(solution)/shard_map/all_gather | solution.py:81
  25.4 398.5 %reduce-scatter.2.cloned.1.call-start = ((), (), s32[]{:S(2)}) async-start(), calls=%async_computation.2 | async-start | bytes 3686400 | tf_op jit(solution)/shard_map/reduce_scatter | solution.py:84
  156.2 8.3 %copy-start.6 = (f32[3200]{0:T(1024)S(1)}, f32[3200]{0:T(1024)}, u32[]{:S(2)}) copy-start(f32[3200]{0:T(1024)} %param.9) | copy-start | bytes 38404
  164.5 18.7 %copy-start.4 = (f32[256]{0:T(256)S(1)}, f32[256]{0:T(256)}, u32[]{:S(2)}) copy-start(f32[256]{0:T(256)} %param.12) | copy-start | bytes 3076
  184.0 120.0 %copy-start.5 = (f32[256]{0:T(256)S(1)}, f32[256]{0:T(256)}, u32[]{:S(2)}) copy-start(f32[256]{0:T(256)} %param.11) | copy-start | bytes 3076
  184.7 121.0 %collective-permute-start = (bf16[256,2,256]{0,2,1:T(8,128)(2,1)}, bf16[256,2,256]{0,2,1:T(8,128)(2,1)}, u32[]{:S(2)}, u32[]{:S(2)}) collective-permute-start(bf16[256,2,256]{0,2,1:T(8,128)(2,1)} %pad_maximum_fusion), channel_id=1, source_target_pairs={{0,16},{8,24},{16,32},{24,40},{32,48},{40,56},{48,64},{56,72},{64,... | collective-permute-start | bytes 786440 | tf_op jit(solution)/shard_map/ppermute | solution.py:14
  289.7 17.0 %collective-permute-start.1 = (bf16[256,2,256]{0,2,1:T(8,128)(2,1)}, bf16[256,2,256]{0,2,1:T(8,128)(2,1)}, u32[]{:S(2)}, u32[]{:S(2)}) collective-permute-start(bf16[256,2,256]{0,2,1:T(8,128)(2,1)} %pad_maximum_fusion), channel_id=1, source_target_pairs={{0,8},{8,16},{16,24},{24,32},{32,40},{40,48},{48,56},{56,64},{64,7... | collective-permute-start | bytes 786440 | tf_op jit(solution)/shard_map/ppermute | solution.py:14
  293.4 14.2 %collective-permute-start.2 = (bf16[256,2,256]{0,2,1:T(8,128)(2,1)}, bf16[256,2,256]{0,2,1:T(8,128)(2,1)}, u32[]{:S(2)}, u32[]{:S(2)}) collective-permute-start(bf16[256,2,256]{0,2,1:T(8,128)(2,1)} %pad_maximum_fusion), channel_id=1, source_target_pairs={{8,0},{16,8},{24,16},{32,24},{40,32},{48,40},{56,48},{64,56},{72,6... | collective-permute-start | bytes 786440 | tf_op jit(solution)/shard_map/ppermute | solution.py:14
  296.2 12.5 %collective-permute-start.3 = (bf16[256,2,256]{0,2,1:T(8,128)(2,1)}, bf16[256,2,256]{0,2,1:T(8,128)(2,1)}, u32[]{:S(2)}, u32[]{:S(2)}) collective-permute-start(bf16[256,2,256]{0,2,1:T(8,128)(2,1)} %pad_maximum_fusion), channel_id=1, source_target_pairs={{16,0},{24,8},{32,16},{40,24},{48,32},{56,40},{64,48},{72,56},{80,... | collective-permute-start | bytes 786440 | tf_op jit(solution)/shard_map/ppermute | solution.py:14
  307.6 3.2 copy-start.1
  318.6 105.3 %copy-start.3 = (f32[400]{0:T(512)S(1)}, f32[400]{0:T(512)}, u32[]{:S(2)}) copy-start(f32[400]{0:T(512)} %param.14) | copy-start | bytes 4804
Sparse Core Ops, SparseCore 0:
  27.6 259.4 all-gather.2
  318.7 105.1 reduce-scatter.1
